TPU v7x, 32 devices: a whole 2x2x4 slice. The times are simulated.
32 devices in a mesh: group: 2 (over x), dom: 16 (over z, y, core).
Axes of the slice: x: 2, y: 2, z: 4, core: 2. Of those that a mesh axis runs over, the one named last changes fastest.
Arguments:
- features: bfloat16 [8192, 512], P(('group', 'dom')), may hold values from -6 to 6
- tile_columns: int32 [32, 2, 4], P(('group', 'dom')), may hold values from 0 to 1
- tile_values: bfloat16 [32, 2, 4, 128, 128], P(('group', 'dom')), as said below
- send_rows: int32 [32, 16, 16], P(('group', 'dom')), may hold values from 0 to 255
- send_count: int32 [32, 16], P(('group', 'dom')), may hold values from 0 to 16, as said below
- ghost_target: int32 [32, 16, 16], P(('group', 'dom')), may hold values from 0 to 255
- query_rows: int32 [32, 512], P(('group', 'dom')), may hold values from 0 to 255
- positive_cand: int32 [32, 512], P(('group', 'dom')), may hold values from 0 to 63
- negative_rows: int32 [32, 32], P(('group', 'dom')), may hold values from 0 to 255
- weight_self: bfloat16 [512, 512], replicated, may hold values from -0.25 to 0.25
- weight_neigh: bfloat16 [512, 512], replicated, may hold values from -0.75 to 0.75
Outputs:
- embeddings: bfloat16 [8192, 512], P(('group', 'dom'))
- weight_grads: bfloat16 [1024, 512], P('dom')
Inputs may be any that keep to these rules, and one draw needn't show every extreme that they name: `send_count`: no device sends rows to its own index of dom; in every group one index of dom receives exactly 16 rows from every other index. `tile_values`: weights are zero or between 0.5 and 1.
All inputs are finite; a program needn't handle non-finite values.
Results may differ from a plain program's by a relative error of at most 0.015.
Values may be sent and summed in bfloat16 or wider, within the bound.
No kernel may reach another device: no remote copies, remote signals or barrier semaphores. Data moves between devices by JAX's collectives and lax.ppermute only.
A program may use at most 64 MiB of HBM per device.

v0:
```python
import math
import jax
import jax.numpy as jnp
from jax import lax
from jax.sharding import PartitionSpec as P

LOSS_FACTOR = 64.0
EPSILON = 1e-05


def score_grads(scores, positive, cand_total, query_total):
    sigma = jax.nn.sigmoid(scores)
    dscore = jnp.where(positive, sigma - 1.0, sigma / (cand_total - 1.0)) * (
        LOSS_FACTOR / query_total
    )
    return dscore.astype(jnp.bfloat16)


def transpose_dot(left, right):
    return lax.dot_general(
        left, right, (((0,), (0,)), ((), ())), preferred_element_type=jnp.float32
    )


def on_device(
    features,
    tile_columns,
    tile_values,
    send_rows,
    send_count,
    ghost_target,
    query_rows,
    positive_cand,
    negative_rows,
    weight_self,
    weight_neigh,
):
    node_count, width = features.shape
    row_blocks, tiles_row, tile_size = (
        tile_values.shape[1],
        tile_values.shape[2],
        tile_values.shape[3],
    )
    slot_count = send_rows.shape[2]
    group_count = lax.axis_size("group")
    score_factor = 1.0 / math.sqrt(width)
    outgoing = features[send_rows[0]]
    flags = (jnp.arange(slot_count, dtype=jnp.int32)[None, :] < send_count[0][:, None]).astype(
        jnp.bfloat16
    )
    received, flags_in = (
        lax.all_to_all(outgoing, "dom", split_axis=0, concat_axis=0, tiled=True),
        lax.all_to_all(flags, "dom", split_axis=0, concat_axis=0, tiled=True),
    )
    blocks = features.reshape(row_blocks, tile_size, width)
    picked = blocks[tile_columns[0]]
    local = jnp.einsum(
        "rtij,rtjd->rid", tile_values[0], picked, preferred_element_type=jnp.float32
    ).reshape(node_count, width)
    row_weight = jnp.sum(tile_values[0].astype(jnp.float32), axis=(1, 3)).reshape(node_count)
    live = flags_in.astype(jnp.float32)
    targets = ghost_target[0].reshape(-1)
    weighted = (received.astype(jnp.float32) * live[:, :, None]).reshape(-1, width)
    ghost_sum = jnp.zeros((node_count, width), jnp.float32).at[targets].add(weighted)
    ghost_count = jnp.zeros((node_count,), jnp.float32).at[targets].add(live.reshape(-1))
    degree = 1.0 + row_weight + ghost_count
    aggregate = ((local + ghost_sum) / degree[:, None]).astype(jnp.bfloat16)
    pre = jnp.dot(features, weight_self, preferred_element_type=jnp.float32) + jnp.dot(
        aggregate, weight_neigh, preferred_element_type=jnp.float32
    )
    scale = lax.rsqrt(jnp.mean(pre * pre, axis=-1, keepdims=True) + EPSILON)
    embeds = (pre * scale).astype(jnp.bfloat16)
    queries = embeds[query_rows[0]]
    own_negs = embeds[negative_rows[0]]
    neg_count = own_negs.shape[0]
    query_total = queries.shape[0]
    cand_total = neg_count * group_count
    targets_pos = positive_cand[0][:, None]
    all_negs = lax.all_gather(own_negs, "group", axis=0, tiled=True)
    scores = score_factor * jnp.dot(queries, all_negs.T, preferred_element_type=jnp.float32)
    positive = targets_pos == jnp.arange(cand_total, dtype=jnp.int32)[None, :]
    dscore = score_grads(scores, positive, cand_total, query_total)
    query_grad = score_factor * jnp.dot(dscore, all_negs, preferred_element_type=jnp.float32)
    neg_grad = lax.psum_scatter(
        (score_factor * transpose_dot(dscore, queries)).astype(jnp.bfloat16),
        "group",
        scatter_dimension=0,
        tiled=True,
    ).astype(jnp.float32)
    emb_grad = jnp.zeros((node_count, width), jnp.float32)
    emb_grad = emb_grad.at[query_rows[0]].add(query_grad)
    emb_grad = emb_grad.at[negative_rows[0]].add(neg_grad)
    inner = jnp.mean(pre * emb_grad, axis=-1, keepdims=True)
    pre_grad = (scale * emb_grad - pre * scale * scale * scale * inner).astype(jnp.bfloat16)
    stacked = jnp.concatenate([features, aggregate], axis=1)
    shard = lax.psum_scatter(
        transpose_dot(stacked, pre_grad), "dom", scatter_dimension=0, tiled=True
    )
    summed = lax.psum(shard.astype(jnp.bfloat16), "group")
    return (embeds, summed)


def solution(mesh):
    placed = (
        P(("group", "dom"), None),
        P(("group", "dom"), None, None),
        P(("group", "dom"), None, None, None, None),
        P(("group", "dom"), None, None),
        P(("group", "dom"), None),
        P(("group", "dom"), None, None),
        P(("group", "dom"), None),
        P(("group", "dom"), None),
        P(("group", "dom"), None),
        P(),
        P(),
    )
    return jax.shard_map(
        on_device,
        mesh=mesh,
        in_specs=placed,
        out_specs=(P(("group", "dom"), None), P("dom", None)),
        check_vma=False,
    )
```

profile of v0, /device:TPU:0, one launch (start us, length us, event | category | flops | bytes accessed | tf_op | source)
XLA Modules:
  0.0 157.0 jit_solution(12821754926774188139)
XLA Ops:
  7.2 1.4 compare_convert_fusion
  8.6 7.4 %all-to-all-start.1 = ((bf16[16,1,16]{2,1,0:T(2,128)(2,1)}), bf16[16,1,16]{2,1,0:T(2,128)(2,1)S(1)}, u32[]{:S(2)}, u32[]{:S(2)}) async-start(bf16[16,1,16]{2,1,0:T(2,128)(2,1)} %compare_convert_fusion), calls=%async_computation.1 | async-start | bytes 16384 | tf_op jit(solution)/shard_map/all_to_all | solution.py:53
  16.0 0.7 fusion.17
  16.7 0.7 compare_select_fusion.3
  17.4 0.8 reshape_squeeze.3
  18.2 1.1 convert_reduce_fusion
  19.3 0.7 compare_select_fusion.1
  20.0 0.7 compare_select_fusion
  20.8 1.4 fusion.19
  22.3 1.9 %gather_fusion.1 = bf16[256,512]{1,0:T(8,128)(2,1)} fusion(bf16[256,512]{1,0:T(8,128)(2,1)S(1)} %copy-done.2, s32[1024]{0:T(1024)S(1)} %pad_clamp_fusion.2), kind=kCustom, calls=%fused_computation.1 | custom fusion | bytes 525312 | tf_op jit(solution)/shard_map/gather | solution.py:47
  24.1 0.6 gather_fusion
  24.8 6.0 %all-to-all-start = ((bf16[16,16,512]{2,1,0:T(8,128)(2,1)}), bf16[16,16,512]{2,1,0:T(8,128)(2,1)S(1)}, u32[]{:S(2)}, u32[]{:S(2)}) async-start(bf16[16,16,512]{2,1,0:T(8,128)(2,1)} %bitcast.10), calls=%async_computation | async-start | bytes 524288 | tf_op jit(solution)/shard_map/all_to_all | solution.py:52
  30.9 0.3 fusion.9
  31.3 2.3 %scatter_fusion.1 = f32[256]{0:T(256)S(1)} fusion(f32[256]{0:T(256)S(1)} %add_bitcast_fusion, s32[256]{0:T(256)S(1)} %bitcast.51, f32[256]{0:T(256)S(1)} %reshape.273), kind=kCustom, calls=%fused_computation.5 | custom fusion | flops 256 | bytes 4096 | tf_op jit(solution)/shard_map/scatter-add | solution.py:65
  33.6 7.2 %all-to-all-done = bf16[16,16,512]{2,1,0:T(8,128)(2,1)S(1)} async-done(((bf16[16,16,512]{2,1,0:T(8,128)(2,1)}), bf16[16,16,512]{2,1,0:T(8,128)(2,1)S(1)}, u32[]{:S(2)}, u32[]{:S(2)}) %all-to-all-start) | async-done | bytes 262176 | tf_op jit(solution)/shard_map/all_to_all | solution.py:52
  40.9 2.3 %scatter_fusion = f32[256,512]{1,0:T(8,128)S(1)} fusion(f32[256,512]{1,0:T(8,128)S(1)} %bitcast.46, s32[256]{0:T(256)S(1)} %bitcast.52, f32[256,512]{1,0:T(8,128)S(1)} %bitcast.49), kind=kCustom, calls=%fused_computation.4 | custom fusion | flops 131072 | bytes 1573888 | tf_op jit(solution)/shard_map/scatter-add | solution.py:64
  43.3 0.4 multiply_reduce_fusion.1
  43.9 0.6 gather_fusion.3
  44.5 4.6 %all-gather = bf16[64,512]{1,0:T(8,128)(2,1)S(1)} all-gather(bf16[32,512]{1,0:T(8,128)(2,1)S(1)} %gather_fusion.3), channel_id=2, replica_groups=mesh['group'=2,'dom'=16] {'group'}, dimensions={0}, use_global_device_ids=true | all-gather | bytes 98304 | tf_op jit(solution)/shard_map/all_gather | solution.py:79
  49.1 2.0 %gather_fusion.2 = bf16[512,512]{1,0:T(8,128)(2,1)S(1)} fusion(bf16[256,512]{1,0:T(8,128)(2,1)S(1)} %multiply_convert_fusion, s32[1024]{0:T(1024)S(1)} %pad_clamp_fusion.1), kind=kCustom, calls=%fused_computation.2 | custom fusion | bytes 1050624 | tf_op jit(solution)/shard_map/gather | solution.py:73
  51.1 0.3 multiply_convert_fusion.1
  51.4 0.8 fusion.4
  52.3 0.3 convolution_multiply_fusion
  52.6 3.7 %scatter_custom_fusion.2 = f32[256,512]{1,0:T(8,128)S(1)} fusion(s32[512]{0:T(512)S(1)} %bitcast.54, f32[512,512]{1,0:T(8,128)S(1)} %convolution_multiply_fusion, f32[]{:T(128)} %constant.14.clone.1), kind=kCustom, calls=%fused_computation.31 | custom fusion | flops 262144 | bytes 524292 | tf_op jit(solution)/shard_map/scatter-add | solution.py:91
  56.4 4.3 %reduce-scatter.3.cloned.1.call-done = bf16[32,512]{1,0:T(8,128)(2,1)} async-done(((bf16[64,512]{1,0:T(8,128)(2,1)}), bf16[32,512]{1,0:T(8,128)(2,1)}) %reduce-scatter.3.cloned.1.call-update) | async-done | bytes 32784 | tf_op jit(solution)/shard_map/reduce_scatter | solution.py:84
  60.6 1.2 scatter_custom_fusion.3
  61.9 0.1 multiply_reduce_fusion
  62.0 2.0 %fusion.5 = f32[1024,512]{1,0:T(8,128)} fusion(bf16[256,512]{1,0:T(8,128)(2,1)S(1)} %divide_convert_fusion, bf16[256,512]{1,0:T(8,128)(2,1)S(1)} %copy-done.2, f32[256,512]{1,0:T(8,128)S(1)} %scatter_custom_fusion.3, f32[256,512]{1,0:T(8,128)S(1)} %get-tuple-element.3, f32[256]{0:T(256)S(1)} %broadcast_multiply_fusion, f32[256]{0:T(256)S(1)} %add_rsqrt_fusion), kind=kOutput, calls=%fused_computation.17 | convolution fusion | flops 270401536 | bytes 3672064 | tf_op jit(solution)/shard_map/dot_general | solution.py:20
  64.0 62.2 %reduce-scatter.5.cloned.1.call-done = f32[64,512]{1,0:T(8,128)} async-done(((f32[1024,512]{1,0:T(8,128)}), f32[64,512]{1,0:T(8,128)}) %reduce-scatter.5.cloned.1.call-update) | async-done | bytes 131088 | tf_op jit(solution)/shard_map/reduce_scatter | solution.py:96
  126.2 1.5 convert_element_type.66
  127.8 21.2 %all-reduce.2.cloned.1.call-done = bf16[64,512]{1,0:T(8,128)(2,1)} async-done(((bf16[64,512]{1,0:T(8,128)(2,1)}), bf16[64,512]{1,0:T(8,128)(2,1)}) %all-reduce.2.cloned.1.call-update) | async-done | bytes 65552 | tf_op jit(solution)/shard_map/psum | solution.py:99
  149.0 1.5 copy.18
  (33 shorter events, 0.9 us)
Async XLA Ops:
  7.2 36.2 %copy-start = (bf16[512,512]{1,0:T(8,128)(2,1)S(1)}, bf16[512,512]{1,0:T(8,128)(2,1)}, u32[]{:S(2)}) copy-start(bf16[512,512]{1,0:T(8,128)(2,1)} %param.21) | copy-start | bytes 1572868
  7.2 15.1 %copy-start.2 = (bf16[256,512]{1,0:T(8,128)(2,1)S(1)}, bf16[256,512]{1,0:T(8,128)(2,1)}, u32[]{:S(2)}) copy-start(bf16[256,512]{1,0:T(8,128)(2,1)} %param.11) | copy-start | bytes 786436
  8.6 16.1 %all-to-all-start.1 = ((bf16[16,1,16]{2,1,0:T(2,128)(2,1)}), bf16[16,1,16]{2,1,0:T(2,128)(2,1)S(1)}, u32[]{:S(2)}, u32[]{:S(2)}) async-start(bf16[16,1,16]{2,1,0:T(2,128)(2,1)} %compare_convert_fusion), calls=%async_computation.1 | async-start | bytes 16384 | tf_op jit(solution)/shard_map/all_to_all | solution.py:53
  22.3 8.6 %copy-start.3 = (bf16[1,2,4,128,128]{4,3,2,1,0:T(8,128)(2,1)S(1)}, bf16[1,2,4,128,128]{4,3,2,1,0:T(8,128)(2,1)}, u32[]{:S(2)}) copy-start(bf16[1,2,4,128,128]{4,3,2,1,0:T(8,128)(2,1)} %param.13) | copy-start | bytes 786436
  24.8 16.0 %all-to-all-start = ((bf16[16,16,512]{2,1,0:T(8,128)(2,1)}), bf16[16,16,512]{2,1,0:T(8,128)(2,1)S(1)}, u32[]{:S(2)}, u32[]{:S(2)}) async-start(bf16[16,16,512]{2,1,0:T(8,128)(2,1)} %bitcast.10), calls=%async_computation | async-start | bytes 524288 | tf_op jit(solution)/shard_map/all_to_all | solution.py:52
  30.8 29.9 %reduce-scatter.3.cloned.1.call-start = ((), (), s32[]{:S(2)}) async-start(), calls=%async_computation.4 | async-start | bytes 98304 | tf_op jit(solution)/shard_map/reduce_scatter | solution.py:84
  43.9 7.2 %copy-start.1 = (bf16[256,512]{1,0:T(8,128)(2,1)}, bf16[256,512]{1,0:T(8,128)(2,1)S(1)}, u32[]{:S(2)}) copy-start(bf16[256,512]{1,0:T(8,128)(2,1)S(1)} %multiply_convert_fusion) | copy-start | bytes 786436
  49.1 2.0 %copy-start.4 = (s32[1,512]{1,0:T(1,128)S(1)}, s32[1,512]{1,0:T(1,128)}, u32[]{:S(2)}) copy-start(s32[1,512]{1,0:T(1,128)} %param.18) | copy-start | bytes 6148
  52.3 74.0 %reduce-scatter.5.cloned.1.call-start = ((), (), s32[]{:S(2)}) async-start(), calls=%async_computation.5 | async-start | bytes 2228224 | tf_op jit(solution)/shard_map/reduce_scatter | solution.py:96
  64.0 85.0 %all-reduce.2.cloned.1.call-start = ((), (), s32[]{:S(2)}) async-start(), calls=%async_computation.6 | async-start | bytes 131072 | tf_op jit(solution)/shard_map/psum | solution.py:99
Sparse Core Ops, SparseCore 0:
  52.4 8.1 reduce-scatter.2
  64.4 61.8 reduce-scatter.4
  129.1 19.8 all-reduce.1
where the time goes:
time: 158 us; the launch traced here: 157 us
  waiting for transfers between devices  94.9 us (60%)
  other arithmetic  16.8 us (11%)
  between operations  14 us (9%)
  starting transfers between devices  13.6 us (9%)
  local copies, waits for them, and re-layouts  7.58 us (5%)
  matrix products  5.54 us (4%)
  blocking collectives  4.58 us (3%)
    reduce_scatter x1, waiting for transfers between devices, on_device(): lax.psum_scatter(transpose_dot(stacked, pre_grad), 'dom', scatter_dimensi...  62.2 us
    psum x1, waiting for transfers between devices, on_device(): summed = lax.psum(shard.astype(jnp.bfloat16), 'group')  21.2 us
    all_to_all x1, starting transfers between devices, on_device(): lax.all_to_all(flags, 'dom', split_axis=0, concat_axis=0, tiled=True)  7.41 us
    all_to_all x1, waiting for transfers between devices, on_device(): lax.all_to_all(outgoing, 'dom', split_axis=0, concat_axis=0, tiled=True)  7.18 us
    all_to_all x1, starting transfers between devices, on_device(): lax.all_to_all(outgoing, 'dom', split_axis=0, concat_axis=0, tiled=True)  6.02 us
    all_gather x1, blocking collectives, on_device(): all_negs = lax.all_gather(own_negs, 'group', axis=0, tiled=True)  4.58 us
    reduce_scatter x1, waiting for transfers between devices, on_device(): lax.psum_scatter((score_factor * transpose_dot(dscore, queries)).astype(j...  4.28 us
    scatter-add x1, other arithmetic, on_device(): emb_grad = emb_grad.at[query_rows[0]].add(query_grad)  3.71 us
  transfers between devices with their start and end apart: 5, of which 4 were waited for; matrix products, arithmetic and copies ran while one was open for 10% of the time, Pallas kernels for 0%

commit v1 on v0

--- a/solution.py
+++ b/solution.py
@@ -6,6 +6,22 @@
 
 LOSS_FACTOR = 64.0
 EPSILON = 1e-05
+
+
+def swapped_with_each(array, axis, split, join):
+    ways, here = (lax.axis_size(axis), lax.axis_index(axis))
+    width = array.shape[split] // ways
+    lengths = list(array.shape)
+    lengths[split] = width
+    height = lengths[join]
+    lengths[join] = height * ways
+    full = jnp.zeros(lengths, array.dtype)
+    for mask in range(ways):
+        part = lax.dynamic_slice_in_dim(array, (here ^ mask) * width, width, axis=split)
+        if mask:
+            part = lax.ppermute(part, axis, [(d, d ^ mask) for d in range(ways)])
+        full = lax.dynamic_update_slice_in_dim(full, part, (here ^ mask) * height, axis=join)
+    return full
 
 
 def score_grads(scores, positive, cand_total, query_total):
@@ -49,7 +65,7 @@
         jnp.bfloat16
     )
     received, flags_in = (
-        lax.all_to_all(outgoing, "dom", split_axis=0, concat_axis=0, tiled=True),
+        swapped_with_each(outgoing, "dom", 0, 0),
         lax.all_to_all(flags, "dom", split_axis=0, concat_axis=0, tiled=True),
     )
     blocks = features.reshape(row_blocks, tile_size, width)

time: 158 us -> 201 us (1.27)
  waiting for transfers between devices: 94.9 us -> 123 us
  starting transfers between devices: 13.6 us -> 25.2 us
  local copies, waits for them, and re-layouts: 7.58 us -> 11.7 us
    ppermute x0 -> x15, waiting for transfers between devices: none -> 33 us  [swapped_with_each(): part = lax.ppermute(part, axis, [(d, d ^ mask) for d in range(ways)])]
    ppermute x0 -> x15, starting transfers between devices: none -> 17.7 us  [swapped_with_each(): part = lax.ppermute(part, axis, [(d, d ^ mask) for d in range(ways)])]
    all_to_all x1 -> x0, waiting for transfers between devices: 7.18 us -> none  [on_device(): lax.all_to_all(outgoing, 'dom', split_axis=0, concat_axis=0, tiled=True)]
    all_to_all x1 -> x0, starting transfers between devices: 6.02 us -> none  [on_device(): lax.all_to_all(outgoing, 'dom', split_axis=0, concat_axis=0, tiled=True)]
    dynamic_update_slice x0 -> x15, local copies, waits for them, and re-layouts: none -> 3.63 us  [swapped_with_each(): lax.dynamic_update_slice_in_dim(full, part, (here ^ mask) * height, axis=...]
    reduce_scatter x1, waiting for transfers between devices: 4.28 us -> 6.99 us  [on_device(): lax.psum_scatter((score_factor * transpose_dot(dscore, queries)).astype(j...]
  transfers between devices with their start and end apart: 5 -> 19, of which waited for: 4 -> 13; matrix products, arithmetic and copies ran while one was open for 10% -> 9% of each run, Pallas kernels for 0% -> 0%
where the time goes in v1:
time: 201 us; the launch traced here: 200 us
  waiting for transfers between devices  123 us (61%)
  starting transfers between devices  25.2 us (13%)
  other arithmetic  16.4 us (8%)
  between operations  14.2 us (7%)
  local copies, waits for them, and re-layouts  11.7 us (6%)
  blocking collectives  4.58 us (2%)
  matrix products  4.4 us (2%)
    reduce_scatter x1, waiting for transfers between devices, on_device(): lax.psum_scatter(transpose_dot(stacked, pre_grad), 'dom', scatter_dimensi...  62.2 us
    ppermute x15, waiting for transfers between devices, swapped_with_each(): part = lax.ppermute(part, axis, [(d, d ^ mask) for d in range(ways)])  33 us
    psum x1, waiting for transfers between devices, on_device(): summed = lax.psum(shard.astype(jnp.bfloat16), 'group')  21.1 us
    ppermute x15, starting transfers between devices, swapped_with_each(): part = lax.ppermute(part, axis, [(d, d ^ mask) for d in range(ways)])  17.7 us
    all_to_all x1, starting transfers between devices, on_device(): lax.all_to_all(flags, 'dom', split_axis=0, concat_axis=0, tiled=True)  7.41 us
    reduce_scatter x1, waiting for transfers between devices, on_device(): lax.psum_scatter((score_factor * transpose_dot(dscore, queries)).astype(j...  6.99 us
    all_gather x1, blocking collectives, on_device(): all_negs = lax.all_gather(own_negs, 'group', axis=0, tiled=True)  4.58 us
  transfers between devices with their start and end apart: 19, of which 13 were waited for; matrix products, arithmetic and copies ran while one was open for 9% of the time, Pallas kernels for 0%

profile of v1, /device:TPU:0, one launch (start us, length us, event | category | flops | bytes accessed | tf_op | source)
XLA Modules:
  0.0 199.9 jit_solution(1056349425236211260)
XLA Ops:
  7.3 1.4 compare_convert_fusion
  8.7 7.4 %all-to-all-start = ((bf16[16,1,16]{2,1,0:T(2,128)(2,1)}), bf16[16,1,16]{2,1,0:T(2,128)(2,1)S(1)}, u32[]{:S(2)}, u32[]{:S(2)}) async-start(bf16[16,1,16]{2,1,0:T(2,128)(2,1)} %compare_convert_fusion), calls=%async_computation | async-start | bytes 16384 | tf_op jit(solution)/shard_map/all_to_all | solution.py:69
  17.1 2.2 %gather_fusion.1 = bf16[256,512]{1,0:T(8,128)(2,1)S(1)} fusion(bf16[256,512]{1,0:T(8,128)(2,1)} %param.11, s32[1024]{0:T(1024)S(1)} %pad_clamp_fusion.2), kind=kCustom, calls=%fused_computation.1 | custom fusion | bytes 525312 | tf_op jit(solution)/shard_map/gather | solution.py:63
  20.1 4.3 %collective-permute-start.14 = (bf16[1,16,512]{2,1,0:T(8,128)(2,1)S(1)}, bf16[1,16,512]{2,1,0:T(8,128)(2,1)}, u32[]{:S(2)}, u32[]{:S(2)}) collective-permute-start(bf16[1,16,512]{2,1,0:T(8,128)(2,1)S(1)} %get-tuple-element.2), channel_id=1, source_target_pairs={{0,15},{1,14},{2,13},{3,12},{4,11},{5,10},{6,9},{7,8},{8,7},{9,6},... | collective-permute-start | bytes 49160 | tf_op jit(solution)/shard_map/ppermute | solution.py:22
  24.8 3.2 %collective-permute-start.12 = (bf16[1,16,512]{2,1,0:T(8,128)(2,1)S(1)}, bf16[1,16,512]{2,1,0:T(8,128)(2,1)}, u32[]{:S(2)}, u32[]{:S(2)}) collective-permute-start(bf16[1,16,512]{2,1,0:T(8,128)(2,1)S(1)} %get-tuple-element.4), channel_id=1, source_target_pairs={{0,13},{1,12},{2,15},{3,14},{4,9},{5,8},{6,11},{7,10},{8,5},{9,4},... | collective-permute-start | bytes 49160 | tf_op jit(solution)/shard_map/ppermute | solution.py:22
  32.6 2.3 %scatter_fusion.1 = f32[256]{0:T(256)S(1)} fusion(f32[256]{0:T(256)S(1)} %add_bitcast_fusion, s32[256]{0:T(256)S(1)} %bitcast.52, f32[256]{0:T(256)S(1)} %reshape.273), kind=kCustom, calls=%fused_computation.5 | custom fusion | flops 256 | bytes 4096 | tf_op jit(solution)/shard_map/scatter-add | solution.py:81
  35.0 1.7 collective-permute-start.1
  37.4 1.6 collective-permute-done.1
  39.5 2.9 %collective-permute-done.2 = bf16[1,16,512]{2,1,0:T(8,128)(2,1)S(1)} collective-permute-done((bf16[1,16,512]{2,1,0:T(8,128)(2,1)}, bf16[1,16,512]{2,1,0:T(8,128)(2,1)S(1)}, u32[]{:S(2)}, u32[]{:S(2)}) %collective-permute-start.2) | collective-permute-done | bytes 16416 | tf_op jit(solution)/shard_map/ppermute | solution.py:22
  42.4 3.9 %collective-permute-done.3 = bf16[1,16,512]{2,1,0:T(8,128)(2,1)S(1)} collective-permute-done((bf16[1,16,512]{2,1,0:T(8,128)(2,1)}, bf16[1,16,512]{2,1,0:T(8,128)(2,1)S(1)}, u32[]{:S(2)}, u32[]{:S(2)}) %collective-permute-start.3) | collective-permute-done | bytes 16416 | tf_op jit(solution)/shard_map/ppermute | solution.py:22
  46.3 3.4 %collective-permute-done.4 = bf16[1,16,512]{2,1,0:T(8,128)(2,1)S(1)} collective-permute-done((bf16[1,16,512]{2,1,0:T(8,128)(2,1)}, bf16[1,16,512]{2,1,0:T(8,128)(2,1)S(1)}, u32[]{:S(2)}, u32[]{:S(2)}) %collective-permute-start.4) | collective-permute-done | bytes 16416 | tf_op jit(solution)/shard_map/ppermute | solution.py:22
  49.7 1.1 collective-permute-start.5
  50.8 3.8 %collective-permute-done.5 = bf16[1,16,512]{2,1,0:T(8,128)(2,1)S(1)} collective-permute-done((bf16[1,16,512]{2,1,0:T(8,128)(2,1)}, bf16[1,16,512]{2,1,0:T(8,128)(2,1)S(1)}, u32[]{:S(2)}, u32[]{:S(2)}) %collective-permute-start.5) | collective-permute-done | bytes 16416 | tf_op jit(solution)/shard_map/ppermute | solution.py:22
  54.5 4.3 %collective-permute-done.6 = bf16[1,16,512]{2,1,0:T(8,128)(2,1)S(1)} collective-permute-done((bf16[1,16,512]{2,1,0:T(8,128)(2,1)}, bf16[1,16,512]{2,1,0:T(8,128)(2,1)S(1)}, u32[]{:S(2)}, u32[]{:S(2)}) %collective-permute-start.6) | collective-permute-done | bytes 16416 | tf_op jit(solution)/shard_map/ppermute | solution.py:22
  58.8 2.1 %collective-permute-start.7 = (bf16[1,16,512]{2,1,0:T(8,128)(2,1)S(1)}, bf16[1,16,512]{2,1,0:T(8,128)(2,1)S(1)}, u32[]{:S(2)}, u32[]{:S(2)}) collective-permute-start(bf16[1,16,512]{2,1,0:T(8,128)(2,1)S(1)} %get-tuple-element.9), channel_id=1, source_target_pairs={{0,8},{1,9},{2,10},{3,11},{4,12},{5,13},{6,14},{7,15},{8,0},{9,1},... | collective-permute-start | bytes 49160 | tf_op jit(solution)/shard_map/ppermute | solution.py:22
  61.0 2.5 %collective-permute-done.7 = bf16[1,16,512]{2,1,0:T(8,128)(2,1)S(1)} collective-permute-done((bf16[1,16,512]{2,1,0:T(8,128)(2,1)S(1)}, bf16[1,16,512]{2,1,0:T(8,128)(2,1)S(1)}, u32[]{:S(2)}, u32[]{:S(2)}) %collective-permute-start.7) | collective-permute-done | bytes 16416 | tf_op jit(solution)/shard_map/ppermute | solution.py:22
  64.3 3.2 %collective-permute-done.8 = bf16[1,16,512]{2,1,0:T(8,128)(2,1)S(1)} collective-permute-done((bf16[1,16,512]{2,1,0:T(8,128)(2,1)S(1)}, bf16[1,16,512]{2,1,0:T(8,128)(2,1)S(1)}, u32[]{:S(2)}, u32[]{:S(2)}) %collective-permute-start.8) | collective-permute-done | bytes 16416 | tf_op jit(solution)/shard_map/ppermute | solution.py:22
  67.5 2.9 %collective-permute-start.9 = (bf16[1,16,512]{2,1,0:T(8,128)(2,1)S(1)}, bf16[1,16,512]{2,1,0:T(8,128)(2,1)S(1)}, u32[]{:S(2)}, u32[]{:S(2)}) collective-permute-start(bf16[1,16,512]{2,1,0:T(8,128)(2,1)S(1)} %get-tuple-element.7), channel_id=1, source_target_pairs={{0,10},{1,11},{2,8},{3,9},{4,14},{5,15},{6,12},{7,13},{8,2},{9,3},... | collective-permute-start | bytes 49160 | tf_op jit(solution)/shard_map/ppermute | solution.py:22
  70.4 2.7 %collective-permute-done.9 = bf16[1,16,512]{2,1,0:T(8,128)(2,1)S(1)} collective-permute-done((bf16[1,16,512]{2,1,0:T(8,128)(2,1)S(1)}, bf16[1,16,512]{2,1,0:T(8,128)(2,1)S(1)}, u32[]{:S(2)}, u32[]{:S(2)}) %collective-permute-start.9) | collective-permute-done | bytes 16416 | tf_op jit(solution)/shard_map/ppermute | solution.py:22
  73.2 4.8 %collective-permute-done.10 = bf16[1,16,512]{2,1,0:T(8,128)(2,1)S(1)} collective-permute-done((bf16[1,16,512]{2,1,0:T(8,128)(2,1)S(1)}, bf16[1,16,512]{2,1,0:T(8,128)(2,1)S(1)}, u32[]{:S(2)}, u32[]{:S(2)}) %collective-permute-start.10) | collective-permute-done | bytes 16416 | tf_op jit(solution)/shard_map/ppermute | solution.py:22
  81.0 2.3 %scatter_fusion = f32[256,512]{1,0:T(8,128)S(1)} fusion(f32[256,512]{1,0:T(8,128)S(1)} %bitcast.46, s32[256]{0:T(256)S(1)} %bitcast.53, f32[256,512]{1,0:T(8,128)S(1)} %bitcast.49), kind=kCustom, calls=%fused_computation.4 | custom fusion | flops 131072 | bytes 1573888 | tf_op jit(solution)/shard_map/scatter-add | solution.py:80
  84.6 4.6 %all-gather = bf16[64,512]{1,0:T(8,128)(2,1)S(1)} all-gather(bf16[32,512]{1,0:T(8,128)(2,1)S(1)} %gather_fusion.3), channel_id=2, replica_groups=mesh['group'=2,'dom'=16] {'group'}, dimensions={0}, use_global_device_ids=true | all-gather | bytes 98304 | tf_op jit(solution)/shard_map/all_gather | solution.py:95
  89.2 2.0 gather_fusion.2
  91.5 0.8 fusion.4
  92.8 3.8 %scatter_custom_fusion.2 = f32[256,512]{1,0:T(8,128)S(1)} fusion(s32[512]{0:T(512)} %bitcast.55, f32[512,512]{1,0:T(8,128)S(1)} %convolution_multiply_fusion, f32[]{:T(128)} %constant.11.clone.1), kind=kCustom, calls=%fused_computation.31 | custom fusion | flops 262144 | bytes 524800 | tf_op jit(solution)/shard_map/scatter-add | solution.py:107
  96.6 7.0 %reduce-scatter.3.cloned.1.call-done = bf16[32,512]{1,0:T(8,128)(2,1)} async-done(((bf16[64,512]{1,0:T(8,128)(2,1)}), bf16[32,512]{1,0:T(8,128)(2,1)}) %reduce-scatter.3.cloned.1.call-update) | async-done | bytes 32784 | tf_op jit(solution)/shard_map/reduce_scatter | solution.py:100
  103.6 1.2 scatter_custom_fusion.3
  105.0 1.9 fusion.5
  107.0 62.2 %reduce-scatter.5.cloned.1.call-done = f32[64,512]{1,0:T(8,128)} async-done(((f32[1024,512]{1,0:T(8,128)}), f32[64,512]{1,0:T(8,128)}) %reduce-scatter.5.cloned.1.call-update) | async-done | bytes 131088 | tf_op jit(solution)/shard_map/reduce_scatter | solution.py:112
  169.2 1.5 convert_element_type.66
  170.7 21.1 %all-reduce.2.cloned.1.call-done = bf16[64,512]{1,0:T(8,128)(2,1)} async-done(((bf16[64,512]{1,0:T(8,128)(2,1)}), bf16[64,512]{1,0:T(8,128)(2,1)}) %all-reduce.2.cloned.1.call-update) | async-done | bytes 65552 | tf_op jit(solution)/shard_map/psum | solution.py:115
  191.9 1.5 copy.34
  (92 shorter events, 13.9 us)
Async XLA Ops:
  7.2 76.3 %copy-start = (bf16[512,512]{1,0:T(8,128)(2,1)S(1)}, bf16[512,512]{1,0:T(8,128)(2,1)}, u32[]{:S(2)}) copy-start(bf16[512,512]{1,0:T(8,128)(2,1)} %param.21) | copy-start | bytes 1572868
  7.2 23.3 %copy-start.2 = (bf16[256,512]{1,0:T(8,128)(2,1)S(1)}, bf16[256,512]{1,0:T(8,128)(2,1)}, u32[]{:S(2)}) copy-start(bf16[256,512]{1,0:T(8,128)(2,1)} %param.11) | copy-start | bytes 786436
  7.2 21.3 %copy-start.11 = (s32[1,32]{1,0:T(1,128)S(1)}, s32[1,32]{1,0:T(1,128)}, u32[]{:S(2)}) copy-start(s32[1,32]{1,0:T(1,128)} %param.19) | copy-start | bytes 388
  7.2 21.8 %copy-start.9 = (s32[1,2,4]{2,1,0:T(2,128)S(1)}, s32[1,2,4]{2,1,0:T(2,128)}, u32[]{:S(2)}) copy-start(s32[1,2,4]{2,1,0:T(2,128)} %param.12) | copy-start | bytes 100
  7.2 21.9 %copy-start.7 = (s32[1,16,16]{2,1,0:T(8,128)S(1)}, s32[1,16,16]{2,1,0:T(8,128)}, u32[]{:S(2)}) copy-start(s32[1,16,16]{2,1,0:T(8,128)} %param.16) | copy-start | bytes 3076
  7.2 21.9 %copy-start.3 = (bf16[1,2,4,128,128]{4,3,2,1,0:T(8,128)(2,1)S(1)}, bf16[1,2,4,128,128]{4,3,2,1,0:T(8,128)(2,1)}, u32[]{:S(2)}) copy-start(bf16[1,2,4,128,128]{4,3,2,1,0:T(8,128)(2,1)} %param.13) | copy-start | bytes 786436
  7.2 22.1 %copy-start.8 = (s32[1,512]{1,0:T(1,128)S(1)}, s32[1,512]{1,0:T(1,128)}, u32[]{:S(2)}) copy-start(s32[1,512]{1,0:T(1,128)} %param.17) | copy-start | bytes 6148
  7.2 23.3 %copy-start.4 = (bf16[512,512]{1,0:T(8,128)(2,1)S(1)}, bf16[512,512]{1,0:T(8,128)(2,1)}, u32[]{:S(2)}) copy-start(bf16[512,512]{1,0:T(8,128)(2,1)} %param.20) | copy-start | bytes 1572868
  8.7 23.8 %all-to-all-start = ((bf16[16,1,16]{2,1,0:T(2,128)(2,1)}), bf16[16,1,16]{2,1,0:T(2,128)(2,1)S(1)}, u32[]{:S(2)}, u32[]{:S(2)}) async-start(bf16[16,1,16]{2,1,0:T(2,128)(2,1)} %compare_convert_fusion), calls=%async_computation | async-start | bytes 16384 | tf_op jit(solution)/shard_map/all_to_all | solution.py:69
  16.1 87.5 %reduce-scatter.3.cloned.1.call-start = ((), (), s32[]{:S(2)}) async-start(), calls=%async_computation.3 | async-start | bytes 98304 | tf_op jit(solution)/shard_map/reduce_scatter | solution.py:100
  20.1 60.1 %collective-permute-start.14 = (bf16[1,16,512]{2,1,0:T(8,128)(2,1)S(1)}, bf16[1,16,512]{2,1,0:T(8,128)(2,1)}, u32[]{:S(2)}, u32[]{:S(2)}) collective-permute-start(bf16[1,16,512]{2,1,0:T(8,128)(2,1)S(1)} %get-tuple-element.2), channel_id=1, source_target_pairs={{0,15},{1,14},{2,13},{3,12},{4,11},{5,10},{6,9},{7,8},{8,7},{9,6},... | collective-permute-start | bytes 49160 | tf_op jit(solution)/shard_map/ppermute | solution.py:22
  24.4 55.1 %collective-permute-start.13 = (bf16[1,16,512]{2,1,0:T(8,128)(2,1)S(1)}, bf16[1,16,512]{2,1,0:T(8,128)(2,1)}, u32[]{:S(2)}, u32[]{:S(2)}) collective-permute-start(bf16[1,16,512]{2,1,0:T(8,128)(2,1)S(1)} %get-tuple-element.3), channel_id=1, source_target_pairs={{0,14},{1,15},{2,12},{3,13},{4,10},{5,11},{6,8},{7,9},{8,6},{9,7},... | collective-permute-start | bytes 49160 | tf_op jit(solution)/shard_map/ppermute | solution.py:22
  24.8 54.0 %collective-permute-start.12 = (bf16[1,16,512]{2,1,0:T(8,128)(2,1)S(1)}, bf16[1,16,512]{2,1,0:T(8,128)(2,1)}, u32[]{:S(2)}, u32[]{:S(2)}) collective-permute-start(bf16[1,16,512]{2,1,0:T(8,128)(2,1)S(1)} %get-tuple-element.4), channel_id=1, source_target_pairs={{0,13},{1,12},{2,15},{3,14},{4,9},{5,8},{6,11},{7,10},{8,5},{9,4},... | collective-permute-start | bytes 49160 | tf_op jit(solution)/shard_map/ppermute | solution.py:22
  27.9 50.1 %collective-permute-start.11 = (bf16[1,16,512]{2,1,0:T(8,128)(2,1)S(1)}, bf16[1,16,512]{2,1,0:T(8,128)(2,1)}, u32[]{:S(2)}, u32[]{:S(2)}) collective-permute-start(bf16[1,16,512]{2,1,0:T(8,128)(2,1)S(1)} %get-tuple-element.5), channel_id=1, source_target_pairs={{0,12},{1,13},{2,14},{3,15},{4,8},{5,9},{6,10},{7,11},{8,4},{9,5},... | collective-permute-start | bytes 49160 | tf_op jit(solution)/shard_map/ppermute | solution.py:22
  28.2 6.7 %collective-permute-start = (bf16[1,16,512]{2,1,0:T(8,128)(2,1)}, bf16[1,16,512]{2,1,0:T(8,128)(2,1)}, u32[]{:S(2)}, u32[]{:S(2)}) collective-permute-start(bf16[1,16,512]{2,1,0:T(8,128)(2,1)} %get-tuple-element.16), channel_id=1, source_target_pairs={{0,1},{1,0},{2,3},{3,2},{4,5},{5,4},{6,7},{7,6},{8,9},{9,8},{10,11... | collective-permute-start | bytes 49160 | tf_op jit(solution)/shard_map/ppermute | solution.py:22
  29.3 0.6 copy-start.6
  35.0 4.0 %collective-permute-start.1 = (bf16[1,16,512]{2,1,0:T(8,128)(2,1)}, bf16[1,16,512]{2,1,0:T(8,128)(2,1)S(1)}, u32[]{:S(2)}, u32[]{:S(2)}) collective-permute-start(bf16[1,16,512]{2,1,0:T(8,128)(2,1)} %get-tuple-element.15), channel_id=1, source_target_pairs={{0,2},{1,3},{2,0},{3,1},{4,6},{5,7},{6,4},{7,5},{8,10},{9,11},{10,... | collective-permute-start | bytes 49160 | tf_op jit(solution)/shard_map/ppermute | solution.py:22
  39.0 3.4 %collective-permute-start.2 = (bf16[1,16,512]{2,1,0:T(8,128)(2,1)}, bf16[1,16,512]{2,1,0:T(8,128)(2,1)S(1)}, u32[]{:S(2)}, u32[]{:S(2)}) collective-permute-start(bf16[1,16,512]{2,1,0:T(8,128)(2,1)} %get-tuple-element.14), channel_id=1, source_target_pairs={{0,3},{1,2},{2,1},{3,0},{4,7},{5,6},{6,5},{7,4},{8,11},{9,10},{10,... | collective-permute-start | bytes 49160 | tf_op jit(solution)/shard_map/ppermute | solution.py:22
  42.4 3.9 %collective-permute-start.3 = (bf16[1,16,512]{2,1,0:T(8,128)(2,1)}, bf16[1,16,512]{2,1,0:T(8,128)(2,1)S(1)}, u32[]{:S(2)}, u32[]{:S(2)}) collective-permute-start(bf16[1,16,512]{2,1,0:T(8,128)(2,1)} %get-tuple-element.13), channel_id=1, source_target_pairs={{0,4},{1,5},{2,6},{3,7},{4,0},{5,1},{6,2},{7,3},{8,12},{9,13},{10,... | collective-permute-start | bytes 49160 | tf_op jit(solution)/shard_map/ppermute | solution.py:22
  46.3 3.4 %collective-permute-start.4 = (bf16[1,16,512]{2,1,0:T(8,128)(2,1)}, bf16[1,16,512]{2,1,0:T(8,128)(2,1)S(1)}, u32[]{:S(2)}, u32[]{:S(2)}) collective-permute-start(bf16[1,16,512]{2,1,0:T(8,128)(2,1)} %get-tuple-element.12), channel_id=1, source_target_pairs={{0,5},{1,4},{2,7},{3,6},{4,1},{5,0},{6,3},{7,2},{8,13},{9,12},{10,... | collective-permute-start | bytes 49160 | tf_op jit(solution)/shard_map/ppermute | solution.py:22
  49.7 4.8 %collective-permute-start.5 = (bf16[1,16,512]{2,1,0:T(8,128)(2,1)}, bf16[1,16,512]{2,1,0:T(8,128)(2,1)S(1)}, u32[]{:S(2)}, u32[]{:S(2)}) collective-permute-start(bf16[1,16,512]{2,1,0:T(8,128)(2,1)} %get-tuple-element.11), channel_id=1, source_target_pairs={{0,6},{1,7},{2,4},{3,5},{4,2},{5,3},{6,0},{7,1},{8,14},{9,15},{10,... | collective-permute-start | bytes 49160 | tf_op jit(solution)/shard_map/ppermute | solution.py:22
  54.5 4.3 %collective-permute-start.6 = (bf16[1,16,512]{2,1,0:T(8,128)(2,1)}, bf16[1,16,512]{2,1,0:T(8,128)(2,1)S(1)}, u32[]{:S(2)}, u32[]{:S(2)}) collective-permute-start(bf16[1,16,512]{2,1,0:T(8,128)(2,1)} %get-tuple-element.10), channel_id=1, source_target_pairs={{0,7},{1,6},{2,5},{3,4},{4,3},{5,2},{6,1},{7,0},{8,15},{9,14},{10,... | collective-permute-start | bytes 49160 | tf_op jit(solution)/shard_map/ppermute | solution.py:22
  58.8 4.6 %collective-permute-start.7 = (bf16[1,16,512]{2,1,0:T(8,128)(2,1)S(1)}, bf16[1,16,512]{2,1,0:T(8,128)(2,1)S(1)}, u32[]{:S(2)}, u32[]{:S(2)}) collective-permute-start(bf16[1,16,512]{2,1,0:T(8,128)(2,1)S(1)} %get-tuple-element.9), channel_id=1, source_target_pairs={{0,8},{1,9},{2,10},{3,11},{4,12},{5,13},{6,14},{7,15},{8,0},{9,1},... | collective-permute-start | bytes 49160 | tf_op jit(solution)/shard_map/ppermute | solution.py:22
  63.4 4.1 %collective-permute-start.8 = (bf16[1,16,512]{2,1,0:T(8,128)(2,1)S(1)}, bf16[1,16,512]{2,1,0:T(8,128)(2,1)S(1)}, u32[]{:S(2)}, u32[]{:S(2)}) collective-permute-start(bf16[1,16,512]{2,1,0:T(8,128)(2,1)S(1)} %get-tuple-element.8), channel_id=1, source_target_pairs={{0,9},{1,8},{2,11},{3,10},{4,13},{5,12},{6,15},{7,14},{8,1},{9,0},... | collective-permute-start | bytes 49160 | tf_op jit(solution)/shard_map/ppermute | solution.py:22
  67.5 5.5 %collective-permute-start.9 = (bf16[1,16,512]{2,1,0:T(8,128)(2,1)S(1)}, bf16[1,16,512]{2,1,0:T(8,128)(2,1)S(1)}, u32[]{:S(2)}, u32[]{:S(2)}) collective-permute-start(bf16[1,16,512]{2,1,0:T(8,128)(2,1)S(1)} %get-tuple-element.7), channel_id=1, source_target_pairs={{0,10},{1,11},{2,8},{3,9},{4,14},{5,15},{6,12},{7,13},{8,2},{9,3},... | collective-permute-start | bytes 49160 | tf_op jit(solution)/shard_map/ppermute | solution.py:22
  73.1 5.0 %collective-permute-start.10 = (bf16[1,16,512]{2,1,0:T(8,128)(2,1)S(1)}, bf16[1,16,512]{2,1,0:T(8,128)(2,1)S(1)}, u32[]{:S(2)}, u32[]{:S(2)}) collective-permute-start(bf16[1,16,512]{2,1,0:T(8,128)(2,1)S(1)} %get-tuple-element.6), channel_id=1, source_target_pairs={{0,11},{1,10},{2,9},{3,8},{4,15},{5,14},{6,13},{7,12},{8,3},{9,2},... | collective-permute-start | bytes 49160 | tf_op jit(solution)/shard_map/ppermute | solution.py:22
  83.3 5.9 %copy-start.5 = (s32[1024]{0:T(1024)S(1)}, s32[1024]{0:T(1024)}, u32[]{:S(2)}) copy-start(s32[1024]{0:T(1024)} %pad_clamp_fusion.1) | copy-start | bytes 12292
  84.0 7.2 %copy-start.1 = (bf16[256,512]{1,0:T(8,128)(2,1)}, bf16[256,512]{1,0:T(8,128)(2,1)S(1)}, u32[]{:S(2)}) copy-start(bf16[256,512]{1,0:T(8,128)(2,1)S(1)} %multiply_convert_fusion) | copy-start | bytes 786436
  89.2 2.0 copy-start.10
  92.4 76.7 %reduce-scatter.5.cloned.1.call-start = ((), (), s32[]{:S(2)}) async-start(), calls=%async_computation.4 | async-start | bytes 2228224 | tf_op jit(solution)/shard_map/reduce_scatter | solution.py:112
  106.9 84.9 %all-reduce.2.cloned.1.call-start = ((), (), s32[]{:S(2)}) async-start(), calls=%async_computation.5 | async-start | bytes 131072 | tf_op jit(solution)/shard_map/psum | solution.py:115
Sparse Core Ops, SparseCore 0:
  92.5 11.0 reduce-scatter.2
  107.3 61.7 reduce-scatter.4
  172.0 19.8 all-reduce.1
